TPU v7x, 32 devices: a whole 2x2x4 slice. The times are simulated.
32 devices in a mesh: segment: 2 (over x), blk: 4 (over z), mp: 4 (over y, core).
Axes of the slice: x: 2, y: 2, z: 4, core: 2. Of those that a mesh axis runs over, the one named last changes fastest.
Arguments:
- segment_in: bfloat16 [2, 1024, 4096], P('segment', 'blk'), may hold values from -7.5 to 7.5
- norm_gains: float32 [2, 4096], P('segment'), may hold values from 0.25 to 1.75
- projections: bfloat16 [2, 4096, 2, 2048], P('segment', None, None, 'mp'), may hold values from -2 to 2
- live_counts: int32 [2, 4], P(None, 'blk'), may hold values from 1 to 256, 768 in all within a row
- cotangent: bfloat16 [1024, 4096], P('blk', 'mp'), may hold values from -6 to 6
Outputs:
- segment_out: bfloat16 [2, 1024, 4096], P('segment', 'blk', 'mp')
- state_grads: bfloat16 [2, 1024, 4096], P('segment', 'blk', 'mp')
Inputs may be any that keep to these rules, and one draw needn't show every extreme that they name: `live_counts`: each row sums to 768; every entry is at least 1; each row has an entry equal to 256.
All inputs are finite; a program needn't handle non-finite values. No bound on the sum of `live_counts` on one device may be relied on, other than what follows from the above.
Results may differ from a plain program's by a relative error of at most 0.015.
Values may be sent and summed in bfloat16 or wider, within the bound.
No kernel may reach another device: no remote copies, remote signals or barrier semaphores. Data moves between devices by JAX's collectives and lax.ppermute only.
A program may use at most 128 MiB of HBM per device.

v0:
```python
import jax
import jax.numpy as jnp
from jax import lax
from jax.sharding import PartitionSpec as P

DH = 64
WIN = 4
EPSILON = 1e-06
SCALE = 0.125
NEGATIVE = -1e30


def from_behind(x, axis, by):
    size = lax.axis_size(axis)
    pairs = [(i, i + by) for i in range(size) if 0 <= i + by < size]
    return lax.ppermute(x, axis, pairs)


def normalize(states, gain_row):
    widened = states.astype(jnp.float32)
    spread = jnp.sqrt(jnp.mean(widened * widened, axis=-1, keepdims=True) + EPSILON)
    return ((widened / spread * gain_row).astype(jnp.bfloat16), spread)


def right_product(left, right):
    return lax.dot_general(
        left, right, (((1,), (1,)), ((), ())), preferred_element_type=jnp.float32
    )


def per_device(segment_in, norm_gains, projections, live_counts, cotangent):
    segment_pos = lax.axis_index("segment")
    model_index = lax.axis_index("mp")
    states = segment_in[0]
    gain_row = norm_gains[0]
    row_count, full_width = states.shape
    feature_width = cotangent.shape[1]
    w_primary = projections[0, :, 0, :]
    w_secondary = projections[0, :, 1, :]
    group_width = w_primary.shape[1]
    group_heads = group_width // DH
    normed, spread = normalize(states, gain_row)
    primary = jnp.dot(normed, w_primary, preferred_element_type=jnp.float32).astype(jnp.bfloat16)
    secondary = lax.cond(
        segment_pos == 0,
        lambda: jnp.dot(normed, w_secondary, preferred_element_type=jnp.float32).astype(
            jnp.bfloat16
        ),
        lambda: jnp.zeros_like(primary),
    )
    doc_keys, doc_values = from_behind((primary, secondary), "segment", 1)
    own_block = (doc_keys, doc_values, live_counts[0])
    window = [own_block]
    moving = own_block
    for offset in range(1, WIN):
        moving = from_behind((moving[0], moving[1], moving[2]), "blk", 1)
        window.append(moving)
    position = jnp.arange(row_count, dtype=jnp.int32)
    all_keys = jnp.concatenate([piece[0] for piece in window], 0).reshape(
        WIN * row_count, group_heads, DH
    )
    all_values = jnp.concatenate([piece[1] for piece in window], 0).reshape(
        WIN * row_count, group_heads, DH
    )
    key_live = jnp.concatenate([position < piece[2][0] for piece in window], 0)
    query_live = position < live_counts[1][0]
    query_heads = primary.reshape(row_count, group_heads, DH)
    scores = (
        jnp.einsum("qhd,khd->hqk", query_heads, all_keys, preferred_element_type=jnp.float32)
        * SCALE
    )
    scores = jnp.where(key_live[None, None, :], scores, NEGATIVE)
    row_max = jnp.max(scores, axis=-1, keepdims=True)
    expo = jnp.exp(scores - row_max)
    row_total = jnp.sum(expo, axis=-1, keepdims=True)
    softmax_out = expo / row_total
    weights_low = softmax_out.astype(jnp.bfloat16)
    attended = jnp.einsum(
        "hqk,khd->qhd", weights_low, all_values, preferred_element_type=jnp.float32
    ).astype(jnp.bfloat16)
    attended = jnp.where(query_live[:, None, None], attended, jnp.zeros_like(attended)).reshape(
        row_count, group_width
    )
    projected = lax.cond(
        segment_pos == 1,
        lambda: right_product(attended, w_secondary),
        lambda: jnp.zeros((row_count, full_width), jnp.float32),
    )
    layer_out = lax.psum_scatter(
        projected.astype(jnp.bfloat16), "mp", scatter_dimension=1, tiled=True
    )
    own_normed = lax.dynamic_slice_in_dim(normed, model_index * feature_width, feature_width, 1)
    segment_out = jnp.where(segment_pos == 0, own_normed, layer_out)[None]
    grad_out = jnp.dot(
        lax.all_gather(cotangent, "mp", axis=1, tiled=True),
        w_secondary,
        preferred_element_type=jnp.float32,
    )
    grad_out = grad_out.astype(jnp.bfloat16)
    grad_out = jnp.where(query_live[:, None], grad_out, jnp.zeros_like(grad_out))
    grad_heads = grad_out.reshape(row_count, group_heads, DH)
    grad_probs = jnp.einsum(
        "qhd,khd->hqk", grad_heads, all_values, preferred_element_type=jnp.float32
    )
    row_delta = jnp.sum(softmax_out * grad_probs, axis=-1, keepdims=True)
    grad_scores = (softmax_out * (grad_probs - row_delta)).astype(jnp.bfloat16)
    grad_queries = (
        (
            SCALE
            * jnp.einsum("hqk,khd->qhd", grad_scores, all_keys, preferred_element_type=jnp.float32)
        )
        .astype(jnp.bfloat16)
        .reshape(row_count, group_width)
    )
    key_parts = (
        SCALE
        * jnp.einsum("hqk,qhd->khd", grad_scores, query_heads, preferred_element_type=jnp.float32)
    ).reshape(WIN, row_count, group_width)
    value_parts = jnp.einsum(
        "hqk,qhd->khd", weights_low, grad_heads, preferred_element_type=jnp.float32
    ).reshape(WIN, row_count, group_width)
    key_total = key_parts[WIN - 1]
    value_total = value_parts[WIN - 1]
    for offset in range(WIN - 2, -1, -1):
        arrived = (
            from_behind(key_total.astype(jnp.bfloat16), "blk", -1).astype(key_total.dtype),
            from_behind(value_total.astype(jnp.bfloat16), "blk", -1).astype(value_total.dtype),
        )
        key_total = arrived[0] + key_parts[offset]
        value_total = arrived[1] + value_parts[offset]
    grad_keys = key_total.astype(jnp.bfloat16)
    grad_values = value_total.astype(jnp.bfloat16)
    back_keys, back_values = from_behind((grad_keys, grad_values), "segment", -1)
    partial_grad = lax.cond(
        segment_pos == 0,
        lambda: right_product(back_keys, w_primary) + right_product(back_values, w_secondary),
        lambda: right_product(grad_queries, w_primary),
    )
    widened = states.astype(jnp.float32)
    summed = lax.psum_scatter(
        partial_grad.astype(jnp.bfloat16), "mp", scatter_dimension=1, tiled=True
    ).astype(jnp.float32)
    own_states = lax.dynamic_slice_in_dim(widened, model_index * feature_width, feature_width, 1)
    own_gain = lax.dynamic_slice_in_dim(gain_row, model_index * feature_width, feature_width, 0)
    row_term = lax.psum(jnp.sum(summed * own_gain * own_states, axis=-1, keepdims=True), "mp")
    input_grad = (
        own_gain * summed / spread - own_states * row_term / (full_width * spread**3)
    ).astype(jnp.bfloat16)
    return (segment_out, input_grad[None])


def solution(mesh):
    in_specs = (
        P("segment", "blk", None),
        P("segment", None),
        P("segment", None, None, "mp"),
        P(None, "blk"),
        P("blk", "mp"),
    )
    out_specs = (P("segment", "blk", "mp"), P("segment", "blk", "mp"))
    return jax.shard_map(
        per_device, mesh=mesh, in_specs=in_specs, out_specs=out_specs, check_vma=False
    )
```

profile of v0, /device:TPU:0, one launch (start us, length us, event | category | flops | bytes accessed | tf_op | source)
XLA Modules:
  0.0 235.8 jit_solution(16366591640232580074)
XLA Ops:
  7.2 2.1 fusion.2
  9.3 17.6 %fusion.40 = (bf16[1,4096,1,512]{3,2,1,0:T(2,128)(2,1)}, bf16[1,4096,1,512]{3,2,1,0:T(2,128)(2,1)S(1)}) fusion(bf16[1,4096,2,512]{3,2,1,0:T(2,128)(2,1)} %param.13), kind=kLoop, calls=%fused_computation.70 | loop fusion | bytes 16777216 | tf_op jit(solution)/shard_map/slice | solution.py:38
  27.0 3.3 %copy.45 = bf16[1,4096,1,512]{3,1,2,0:T(8,128)(2,1)} copy(bf16[1,4096,1,512]{3,2,1,0:T(2,128)(2,1)S(1)} %get-tuple-element.63) | data formatting | bytes 8388608
  30.2 2.0 fusion.4
  32.3 4.1 %conditional.3 = (bf16[256,512]{1,0:T(8,128)(2,1)S(1)}) conditional(s32[]{:T(128)} %convert_element_type.110, () %tuple.27, (bf16[256,4096]{1,0:T(8,128)(2,1)}, bf16[4096,512]{1,0:T(8,128)(2,1)}) %tuple.58), branch_computations={%region_1.0_spmd, %region_2.0_spmd} | conditional | flops 1073872896 | bytes 6553608 | solution.py:44
  32.3 4.1 %convolution_convert_fusion = bf16[256,512]{1,0:T(8,128)(2,1)S(1)} fusion(bf16[256,4096]{1,0:T(8,128)(2,1)} %get-tuple-element.42, bf16[4096,512]{1,0:T(8,128)(2,1)} %get-tuple-element.43), kind=kOutput, calls=%fused_computation | convolution fusion | flops 1073872896 | bytes 6553600 | tf_op jit(solution)/shard_map/cond/branch_1_fun/dot_general | solution.py:46
  37.7 4.6 %copy.44 = bf16[1,4096,1,512]{3,1,2,0:T(8,128)(2,1)S(1)} copy(bf16[1,4096,1,512]{3,2,1,0:T(2,128)(2,1)} %get-tuple-element.62) | data formatting | bytes 8388608
  45.6 5.0 %collective-permute-start.1 = (bf16[256,512]{1,0:T(8,128)(2,1)S(1)}, bf16[256,512]{1,0:T(8,128)(2,1)S(1)}, u32[]{:S(2)}, u32[]{:S(2)}) collective-permute-start(bf16[256,512]{1,0:T(8,128)(2,1)S(1)} %collective-permute-done), channel_id=1, source_target_pairs={{0,4},{4,8},{8,12},{1,5},{5,9},{9,13},{2,6},{6,10},{10,14},{3,7},{... | collective-permute-start | bytes 786440 | tf_op jit(solution)/shard_map/ppermute | solution.py:16
  50.6 1.5 collective-permute-done.7
  52.0 4.3 %collective-permute-start.8 = (bf16[256,512]{1,0:T(8,128)(2,1)S(1)}, bf16[256,512]{1,0:T(8,128)(2,1)S(1)}, u32[]{:S(2)}, u32[]{:S(2)}) collective-permute-start(bf16[256,512]{1,0:T(8,128)(2,1)S(1)} %collective-permute-done.7), channel_id=1, source_target_pairs={{0,4},{4,8},{8,12},{1,5},{5,9},{9,13},{2,6},{6,10},{10,14},{3,7},{... | collective-permute-start | bytes 786440 | tf_op jit(solution)/shard_map/ppermute | solution.py:16
  57.0 4.0 %collective-permute-start.4 = (s32[1]{0:T(128)}, s32[1]{0:T(128)}, u32[]{:S(2)}, u32[]{:S(2)}) collective-permute-start(s32[1]{0:T(128)} %bitcast.8), channel_id=1, source_target_pairs={{0,4},{4,8},{8,12},{1,5},{5,9},{9,13},{2,6},{6,10},{10,14},{3,7},{... | collective-permute-start | bytes 20 | tf_op jit(solution)/shard_map/ppermute | solution.py:16
  61.0 3.7 %collective-permute-start.2 = (bf16[256,512]{1,0:T(8,128)(2,1)S(1)}, bf16[256,512]{1,0:T(8,128)(2,1)}, u32[]{:S(2)}, u32[]{:S(2)}) collective-permute-start(bf16[256,512]{1,0:T(8,128)(2,1)S(1)} %collective-permute-done.1), channel_id=1, source_target_pairs={{0,4},{4,8},{8,12},{1,5},{5,9},{9,13},{2,6},{6,10},{10,14},{3,7},{... | collective-permute-start | bytes 786440 | tf_op jit(solution)/shard_map/ppermute | solution.py:16
  65.4 2.0 collective-permute-start.9
  68.1 3.2 %collective-permute-start.5 = (s32[1]{0:T(128)}, s32[1]{0:T(128)}, u32[]{:S(2)}, u32[]{:S(2)}) collective-permute-start(s32[1]{0:T(128)} %collective-permute-done.4), channel_id=1, source_target_pairs={{0,4},{4,8},{8,12},{1,5},{5,9},{9,13},{2,6},{6,10},{10,14},{3,7},{... | collective-permute-start | bytes 20 | tf_op jit(solution)/shard_map/ppermute | solution.py:16
  71.9 3.8 %collective-permute-start.3 = (bf16[256,512]{1,0:T(8,128)(2,1)}, bf16[256,512]{1,0:T(8,128)(2,1)S(1)}, u32[]{:S(2)}, u32[]{:S(2)}) collective-permute-start(bf16[256,512]{1,0:T(8,128)(2,1)} %collective-permute-done.2), channel_id=1, source_target_pairs={{0,4},{4,8},{8,12},{1,5},{5,9},{9,13},{2,6},{6,10},{10,14},{3,7},{... | collective-permute-start | bytes 786440 | tf_op jit(solution)/shard_map/ppermute | solution.py:16
  76.5 4.2 %collective-permute-start.6 = (s32[1]{0:T(128)}, s32[1]{0:T(128)}, u32[]{:S(2)}, u32[]{:S(2)}) collective-permute-start(s32[1]{0:T(128)} %collective-permute-done.5), channel_id=1, source_target_pairs={{0,4},{4,8},{8,12},{1,5},{5,9},{9,13},{2,6},{6,10},{10,14},{3,7},{... | collective-permute-start | bytes 20 | tf_op jit(solution)/shard_map/ppermute | solution.py:16
  80.7 2.9 %collective-permute-start.10 = (bf16[256,512]{1,0:T(8,128)(2,1)}, bf16[256,512]{1,0:T(8,128)(2,1)}, u32[]{:S(2)}, u32[]{:S(2)}) collective-permute-start(bf16[256,512]{1,0:T(8,128)(2,1)} %collective-permute-done.9), channel_id=1, source_target_pairs={{0,4},{4,8},{8,12},{1,5},{5,9},{9,13},{2,6},{6,10},{10,14},{3,7},{... | collective-permute-start | bytes 786440 | tf_op jit(solution)/shard_map/ppermute | solution.py:16
  89.7 7.4 %fusion.44 = (f32[8,256]{1,0:T(8,128)S(1)}, f32[8,256,1024]{2,1,0:T(8,128)}) fusion(pred[1024]{0:T(1024)(128)(4,1)S(1)} %pad_add_fusion, bf16[256,8,64]{0,2,1:T(8,128)(2,1)S(1)} %bitcast.110, bf16[1024,8,64]{0,2,1:T(8,128)(2,1)} %bitcast.101), kind=kOutput, calls=%fused_computation.74 | convolution fusion | flops 276825088 | bytes 9708544 | tf_op jit(solution)/shard_map/sub | solution.py:74
  97.0 5.6 %fusion.25 = bf16[256,8,64]{0,2,1:T(8,128)(2,1)} fusion(bf16[1024,8,64]{0,2,1:T(8,128)(2,1)S(1)} %bitcast.112, f32[8,256,1024]{2,1,0:T(8,128)} %get-tuple-element.75, f32[8,256]{1,0:T(8,128)S(1)} %get-tuple-element.74), kind=kOutput, calls=%fused_computation.35 | convolution fusion | flops 272760832 | bytes 9707520 | tf_op jit(solution)/shard_map/hqk,khd->qhd/dot_general | solution.py:78
  102.6 1.6 conditional.4
  102.6 1.6 broadcast.53
  104.3 4.8 %fusion.29 = bf16[256,512]{1,0:T(8,128)(2,1)} fusion(bf16[256,4096]{1,0:T(8,128)(2,1)} %all-gather.2.cloned.1.call-done, bf16[4096,512]{1,0:T(8,128)(2,1)} %bitcast.97, pred[256]{0:T(512)(128)(4,1)S(1)} %iota_compare_fusion), kind=kOutput, calls=%fused_computation.37 | convolution fusion | flops 1074003968 | bytes 6553856 | tf_op jit(solution)/shard_map/dot_general | solution.py:94
  109.1 1.8 copy.31
  110.9 5.1 %multiply_reduce_fusion = (f32[8,256]{1,0:T(8,128)S(1)}, f32[8,256,1024]{2,1,0:T(8,128)S(1)}) fusion(f32[8,256,1024]{2,1,0:T(8,128)} %get-tuple-element.75, f32[8,256]{1,0:T(8,128)S(1)} %get-tuple-element.74, bf16[256,8,64]{0,2,1:T(8,128)(2,1)} %bitcast.117, bf16[1024,8,64]{0,2,1:T(8,128)(2,1)S(1)} %bitcast.113), kind=kOutput, calls=%fused_computation.6 | convolution fusion | flops 274724864 | bytes 18104320 | tf_op jit(solution)/shard_map/qhd,khd->hqk/dot_general | solution.py:102
  118.5 2.0 copy-done.3
  124.3 4.5 %fusion.15 = f32[1024,8,64]{0,2,1:T(8,128)S(1)} fusion(bf16[256,8,64]{0,2,1:T(8,128)(2,1)S(1)} %bitcast.118, f32[8,256,1024]{2,1,0:T(8,128)} %get-tuple-element.75, f32[8,256]{1,0:T(8,128)S(1)} %get-tuple-element.74), kind=kOutput, calls=%fused_computation.29 | convolution fusion | flops 272629760 | bytes 10756096 | tf_op jit(solution)/shard_map/hqk,qhd->khd/dot_general | solution.py:119
  132.5 2.5 %fusion.42 = (f32[256,8,64]{0,2,1:T(8,128)S(1)}, f32[256,8,64]{0,2,1:T(8,128)}, f32[256,8,64]{0,2,1:T(8,128)}) fusion(f32[1024,8,64]{0,2,1:T(8,128)} %copy-done.5), kind=kLoop, calls=%fused_computation.72 | loop fusion | bytes 3145728 | tf_op jit(solution)/shard_map/slice | solution.py:129
  139.9 1.8 collective-permute-done.15
  141.8 1.7 add_convert_fusion.2
  143.5 1.5 collective-permute-start.16
  145.0 2.2 copy.34
  147.2 2.0 copy.38
  152.6 1.5 collective-permute-done.16
  154.1 1.9 add_convert_fusion.1
  157.2 2.0 copy.35
  159.3 2.0 copy.39
  167.0 3.6 %fusion.28 = bf16[256,8,64]{0,2,1:T(8,128)(2,1)S(1)} fusion(bf16[1024,8,64]{0,2,1:T(8,128)(2,1)S(1)} %bitcast.102, bf16[8,256,1024]{2,1,0:T(8,128)(2,1)} %copy-done.3), kind=kOutput, calls=%fused_computation.36 | convolution fusion | flops 268697600 | bytes 5505024 | tf_op jit(solution)/shard_map/hqk,khd->qhd/dot_general | solution.py:110
  170.6 7.4 %collective-permute-done.14 = bf16[256,512]{1,0:T(8,128)(2,1)S(1)} collective-permute-done((bf16[256,512]{1,0:T(8,128)(2,1)S(1)}, bf16[256,512]{1,0:T(8,128)(2,1)S(1)}, u32[]{:S(2)}, u32[]{:S(2)}) %collective-permute-start.14) | collective-permute-done | bytes 262176 | tf_op jit(solution)/shard_map/ppermute | solution.py:16
  178.0 2.8 %collective-permute-done.18 = bf16[256,512]{1,0:T(8,128)(2,1)S(1)} collective-permute-done((bf16[256,512]{1,0:T(8,128)(2,1)S(1)}, bf16[256,512]{1,0:T(8,128)(2,1)S(1)}, u32[]{:S(2)}, u32[]{:S(2)}) %collective-permute-start.18) | collective-permute-done | bytes 262176 | tf_op jit(solution)/shard_map/ppermute | solution.py:16
  180.8 6.1 %conditional.5 = (bf16[256,4096]{1,0:T(8,128)(2,1)}) conditional(s32[]{:T(128)} %convert_element_type.110, (bf16[256,8,64]{0,2,1:T(8,128)(2,1)S(1)}, bf16[4096,512]{1,0:T(8,128)(2,1)S(1)}) %tuple.56, (bf16[256,512]{1,0:T(8,128)(2,1)S(1)}, bf16[4096,512]{1,0:T(8,128)(2,1)S(1)}, bf16[256,512]{1,0:T(8,128)(2,1)S(1)}, ...), branch_computations={%region_9.10_spmd, %region_10.11_spmd} | conditional | flops 2149580800 | bytes 39321720 | solution.py:134
  181.6 2.4 %fusion.46 = f32[256,4096]{1,0:T(8,128)S(1)} fusion(bf16[256,512]{1,0:T(8,128)(2,1)} %copy-done.10, bf16[4096,512]{1,0:T(8,128)(2,1)S(1)} %get-tuple-element.51), kind=kOutput, calls=%fused_computation.76 | convolution fusion | flops 1073741824 | bytes 8650752 | tf_op jit(solution)/shard_map/cond/branch_1_fun/dot_general | solution.py:26
  184.1 2.8 %convolution_add_fusion = bf16[256,4096]{1,0:T(8,128)(2,1)} fusion(f32[256,4096]{1,0:T(8,128)S(1)} %fusion.46, bf16[256,512]{1,0:T(8,128)(2,1)S(1)} %copy-done.17, bf16[4096,512]{1,0:T(8,128)(2,1)S(1)} %copy-done.2), kind=kOutput, calls=%fused_computation.1 | convolution fusion | flops 1075838976 | bytes 10747904 | tf_op jit(solution)/shard_map/cond/branch_1_fun/dot_general | solution.py:26
  186.9 2.5 %convert_element_type.106 = f32[1,256,4096]{2,1,0:T(8,128)} convert(bf16[1,256,4096]{2,1,0:T(8,128)(2,1)S(1)} %copy-done.4) | non-fusion elementwise | flops 1048576 | bytes 6291456 | tf_op jit(solution)/shard_map/convert_element_type | solution.py:20
  189.4 2.0 select_bitcast_fusion
  191.5 28.0 %reduce-scatter.5.cloned.1.call-done = bf16[256,1024]{1,0:T(8,128)(2,1)} async-done(((bf16[256,4096]{1,0:T(8,128)(2,1)}), bf16[256,1024]{1,0:T(8,128)(2,1)}) %reduce-scatter.5.cloned.1.call-update) | async-done | bytes 524304 | tf_op jit(solution)/shard_map/reduce_scatter | solution.py:140
  219.5 1.6 fusion.30
  221.1 5.8 %psum.7 = f32[256]{0:T(256)S(1)} all-reduce(f32[256]{0:T(256)S(1)} %fusion.30), channel_id=1, replica_groups=mesh['segment'=2,'blk'=4,'mp'=4] {'mp'}, use_global_device_ids=true, to_apply=%region_13.14 | all-reduce | flops 256 | bytes 2048 | tf_op jit(solution)/shard_map/psum | solution.py:145
  226.8 2.4 %fusion.36 = bf16[1,256,1024]{2,1,0:T(8,128)(2,1)} fusion(f32[256]{0:T(256)S(1)} %get-tuple-element.70, f32[256]{0:T(256)S(1)} %psum.7, f32[1,256,4096]{2,1,0:T(8,128)} %convert_element_type.106, s32[]{:T(128)S(6)} %select_n.27, f32[256]{0:T(256)S(1)} %get-tuple-element.71, bf16[256,1024]{1,0:T(8,128)(2,1)} %reduce-scatter.5.cloned.1.call-done, ...), kind=kLoop, calls=%fused_computation.57 | loop fusion | flops 1835008 | bytes 2104324 | tf_op jit(solution)/shard_map/broadcast_in_dim | solution.py:149
  (104 shorter events, 40.1 us)
Async XLA Ops:
  7.2 97.1 %all-gather.2.cloned.1.call-start = ((), (), s32[]{:S(2)}) async-start(), calls=%async_computation.3 | async-start | bytes 2621440 | tf_op jit(solution)/shard_map/all_gather | solution.py:95
  26.9 3.3 %copy-start.4 = (bf16[1,256,4096]{2,1,0:T(8,128)(2,1)S(1)}, bf16[1,256,4096]{2,1,0:T(8,128)(2,1)}, u32[]{:S(2)}) copy-start(bf16[1,256,4096]{2,1,0:T(8,128)(2,1)} %param.11) | copy-start | bytes 6291460
  26.9 3.3 %copy-start.18 = (f32[1,4096]{1,0:T(1,128)S(1)}, f32[1,4096]{1,0:T(1,128)}, u32[]{:S(2)}) copy-start(f32[1,4096]{1,0:T(1,128)} %param.12) | copy-start | bytes 49156
  36.3 9.2 %collective-permute-start = (bf16[256,512]{1,0:T(8,128)(2,1)S(1)}, bf16[256,512]{1,0:T(8,128)(2,1)S(1)}, u32[]{:S(2)}, u32[]{:S(2)}) collective-permute-start(bf16[256,512]{1,0:T(8,128)(2,1)S(1)} %get-tuple-element.78), channel_id=1, source_target_pairs={{0,16},{1,17},{2,18},{3,19},{4,20},{5,21},{6,22},{7,23},{8,24},{9,... | collective-permute-start | bytes 786440 | tf_op jit(solution)/shard_map/ppermute | solution.py:16
  37.7 151.8 %reduce-scatter.3.cloned.1.call-start = ((), (), s32[]{:S(2)}) async-start(), calls=%async_computation.2 | async-start | bytes 2621440 | tf_op jit(solution)/shard_map/reduce_scatter | solution.py:89
  42.3 1.9 copy-start
  42.4 14.0 %copy-start.19 = (s32[2,1]{0,1:T(1,128)S(1)}, s32[2,1]{0,1:T(1,128)}, u32[]{:S(2)}) copy-start(s32[2,1]{0,1:T(1,128)} %param.14) | copy-start | bytes 28
  44.3 7.8 %collective-permute-start.7 = (bf16[256,512]{1,0:T(8,128)(2,1)S(1)}, bf16[256,512]{1,0:T(8,128)(2,1)S(1)}, u32[]{:S(2)}, u32[]{:S(2)}) collective-permute-start(bf16[256,512]{1,0:T(8,128)(2,1)S(1)} %fusion.22), channel_id=1, source_target_pairs={{0,16},{1,17},{2,18},{3,19},{4,20},{5,21},{6,22},{7,23},{8,24},{9,... | collective-permute-start | bytes 786440 | tf_op jit(solution)/shard_map/ppermute | solution.py:16
  45.6 38.7 %copy-start.12 = (bf16[256,512]{1,0:T(8,128)(2,1)}, bf16[256,512]{1,0:T(8,128)(2,1)S(1)}, u32[]{:S(2)}) copy-start(bf16[256,512]{1,0:T(8,128)(2,1)S(1)} %collective-permute-done) | copy-start | bytes 786436
  45.6 15.4 %collective-permute-start.1 = (bf16[256,512]{1,0:T(8,128)(2,1)S(1)}, bf16[256,512]{1,0:T(8,128)(2,1)S(1)}, u32[]{:S(2)}, u32[]{:S(2)}) collective-permute-start(bf16[256,512]{1,0:T(8,128)(2,1)S(1)} %collective-permute-done), channel_id=1, source_target_pairs={{0,4},{4,8},{8,12},{1,5},{5,9},{9,13},{2,6},{6,10},{10,14},{3,7},{... | collective-permute-start | bytes 786440 | tf_op jit(solution)/shard_map/ppermute | solution.py:16
  52.0 15.9 %copy-start.13 = (bf16[256,512]{1,0:T(8,128)(2,1)}, bf16[256,512]{1,0:T(8,128)(2,1)S(1)}, u32[]{:S(2)}) copy-start(bf16[256,512]{1,0:T(8,128)(2,1)S(1)} %collective-permute-done.7) | copy-start | bytes 786436
  52.0 13.3 %collective-permute-start.8 = (bf16[256,512]{1,0:T(8,128)(2,1)S(1)}, bf16[256,512]{1,0:T(8,128)(2,1)S(1)}, u32[]{:S(2)}, u32[]{:S(2)}) collective-permute-start(bf16[256,512]{1,0:T(8,128)(2,1)S(1)} %collective-permute-done.7), channel_id=1, source_target_pairs={{0,4},{4,8},{8,12},{1,5},{5,9},{9,13},{2,6},{6,10},{10,14},{3,7},{... | collective-permute-start | bytes 786440 | tf_op jit(solution)/shard_map/ppermute | solution.py:16
  57.0 11.1 %collective-permute-start.4 = (s32[1]{0:T(128)}, s32[1]{0:T(128)}, u32[]{:S(2)}, u32[]{:S(2)}) collective-permute-start(s32[1]{0:T(128)} %bitcast.8), channel_id=1, source_target_pairs={{0,4},{4,8},{8,12},{1,5},{5,9},{9,13},{2,6},{6,10},{10,14},{3,7},{... | collective-permute-start | bytes 20 | tf_op jit(solution)/shard_map/ppermute | solution.py:16
  61.0 23.3 %copy-start.15 = (bf16[256,512]{1,0:T(8,128)(2,1)}, bf16[256,512]{1,0:T(8,128)(2,1)S(1)}, u32[]{:S(2)}) copy-start(bf16[256,512]{1,0:T(8,128)(2,1)S(1)} %collective-permute-done.1) | copy-start | bytes 786436
  61.0 10.9 %collective-permute-start.2 = (bf16[256,512]{1,0:T(8,128)(2,1)S(1)}, bf16[256,512]{1,0:T(8,128)(2,1)}, u32[]{:S(2)}, u32[]{:S(2)}) collective-permute-start(bf16[256,512]{1,0:T(8,128)(2,1)S(1)} %collective-permute-done.1), channel_id=1, source_target_pairs={{0,4},{4,8},{8,12},{1,5},{5,9},{9,13},{2,6},{6,10},{10,14},{3,7},{... | collective-permute-start | bytes 786440 | tf_op jit(solution)/shard_map/ppermute | solution.py:16
  65.4 18.9 %copy-start.14 = (bf16[256,512]{1,0:T(8,128)(2,1)}, bf16[256,512]{1,0:T(8,128)(2,1)S(1)}, u32[]{:S(2)}) copy-start(bf16[256,512]{1,0:T(8,128)(2,1)S(1)} %collective-permute-done.8) | copy-start | bytes 786436
  65.4 15.3 %collective-permute-start.9 = (bf16[256,512]{1,0:T(8,128)(2,1)S(1)}, bf16[256,512]{1,0:T(8,128)(2,1)}, u32[]{:S(2)}, u32[]{:S(2)}) collective-permute-start(bf16[256,512]{1,0:T(8,128)(2,1)S(1)} %collective-permute-done.8), channel_id=1, source_target_pairs={{0,4},{4,8},{8,12},{1,5},{5,9},{9,13},{2,6},{6,10},{10,14},{3,7},{... | collective-permute-start | bytes 786440 | tf_op jit(solution)/shard_map/ppermute | solution.py:16
  68.1 7.7 %collective-permute-start.5 = (s32[1]{0:T(128)}, s32[1]{0:T(128)}, u32[]{:S(2)}, u32[]{:S(2)}) collective-permute-start(s32[1]{0:T(128)} %collective-permute-done.4), channel_id=1, source_target_pairs={{0,4},{4,8},{8,12},{1,5},{5,9},{9,13},{2,6},{6,10},{10,14},{3,7},{... | collective-permute-start | bytes 20 | tf_op jit(solution)/shard_map/ppermute | solution.py:16
  71.9 12.4 %collective-permute-start.3 = (bf16[256,512]{1,0:T(8,128)(2,1)}, bf16[256,512]{1,0:T(8,128)(2,1)S(1)}, u32[]{:S(2)}, u32[]{:S(2)}) collective-permute-start(bf16[256,512]{1,0:T(8,128)(2,1)} %collective-permute-done.2), channel_id=1, source_target_pairs={{0,4},{4,8},{8,12},{1,5},{5,9},{9,13},{2,6},{6,10},{10,14},{3,7},{... | collective-permute-start | bytes 786440 | tf_op jit(solution)/shard_map/ppermute | solution.py:16
  76.5 7.1 %collective-permute-start.6 = (s32[1]{0:T(128)}, s32[1]{0:T(128)}, u32[]{:S(2)}, u32[]{:S(2)}) collective-permute-start(s32[1]{0:T(128)} %collective-permute-done.5), channel_id=1, source_target_pairs={{0,4},{4,8},{8,12},{1,5},{5,9},{9,13},{2,6},{6,10},{10,14},{3,7},{... | collective-permute-start | bytes 20 | tf_op jit(solution)/shard_map/ppermute | solution.py:16
  80.7 6.4 %collective-permute-start.10 = (bf16[256,512]{1,0:T(8,128)(2,1)}, bf16[256,512]{1,0:T(8,128)(2,1)}, u32[]{:S(2)}, u32[]{:S(2)}) collective-permute-start(bf16[256,512]{1,0:T(8,128)(2,1)} %collective-permute-done.9), channel_id=1, source_target_pairs={{0,4},{4,8},{8,12},{1,5},{5,9},{9,13},{2,6},{6,10},{10,14},{3,7},{... | collective-permute-start | bytes 786440 | tf_op jit(solution)/shard_map/ppermute | solution.py:16
  89.7 7.4 %copy-start.9 = (bf16[1024,512]{0,1:T(8,128)(2,1)S(1)}, bf16[1024,512]{0,1:T(8,128)(2,1)}, u32[]{:S(2)}) copy-start(bf16[1024,512]{0,1:T(8,128)(2,1)} %copy.27) | copy-start | bytes 3145732
  104.2 115.3 %reduce-scatter.5.cloned.1.call-start = ((), (), s32[]{:S(2)}) async-start(), calls=%async_computation.4 | async-start | bytes 2621440 | tf_op jit(solution)/shard_map/reduce_scatter | solution.py:140
  110.9 5.1 %slice-start = ((s8[8388608]{0:T(1024)(128)(4,1)}), s8[4194304]{0:T(1024)(128)(4,1)S(1)}, s32[]{:S(2)}) async-start(s8[8388608]{0:T(1024)(128)(4,1)} %bitcast.99), calls=%async_computation.5 | async-start | bytes 8388608
  110.9 6.3 %slice-start.1 = ((s8[8388608]{0:T(1024)(128)(4,1)}), s8[4194304]{0:T(1024)(128)(4,1)S(1)}, s32[]{:S(2)}) async-start(s8[8388608]{0:T(1024)(128)(4,1)} %bitcast.99), calls=%async_computation.6 | async-start | bytes 8388608
  118.5 2.0 copy-start.3
  120.5 3.8 %copy-start.11 = (bf16[256,512]{0,1:T(8,128)(2,1)S(1)}, bf16[256,512]{0,1:T(8,128)(2,1)}, u32[]{:S(2)}) copy-start(bf16[256,512]{0,1:T(8,128)(2,1)} %copy.31) | copy-start | bytes 786436
  121.3 1.4 copy-start.5
  122.9 14.7 %collective-permute-start.11 = (bf16[256,512]{1,0:T(8,128)(2,1)S(1)}, bf16[256,512]{1,0:T(8,128)(2,1)}, u32[]{:S(2)}, u32[]{:S(2)}) collective-permute-start(bf16[256,512]{1,0:T(8,128)(2,1)S(1)} %copy.32), channel_id=1, source_target_pairs={{4,0},{8,4},{12,8},{5,1},{9,5},{13,9},{6,2},{10,6},{14,10},{7,3},{... | collective-permute-start | bytes 786440 | tf_op jit(solution)/shard_map/ppermute | solution.py:16
  128.8 1.4 copy-start.7
  131.0 3.9 %copy-start.8 = (f32[1024,8,64]{0,2,1:T(8,128)S(1)}, f32[1024,8,64]{0,2,1:T(8,128)}, u32[]{:S(2)}) copy-start(f32[1024,8,64]{0,2,1:T(8,128)} %copy-done.7) | copy-start | bytes 6291460
  131.0 10.7 %collective-permute-start.15 = (bf16[256,512]{1,0:T(8,128)(2,1)}, bf16[256,512]{1,0:T(8,128)(2,1)}, u32[]{:S(2)}, u32[]{:S(2)}) collective-permute-start(bf16[256,512]{1,0:T(8,128)(2,1)} %copy.36), channel_id=1, source_target_pairs={{4,0},{8,4},{12,8},{5,1},{9,5},{13,9},{6,2},{10,6},{14,10},{7,3},{... | collective-permute-start | bytes 786440 | tf_op jit(solution)/shard_map/ppermute | solution.py:16
  138.6 11.5 %collective-permute-start.12 = (bf16[256,512]{1,0:T(8,128)(2,1)S(1)}, bf16[256,512]{1,0:T(8,128)(2,1)}, u32[]{:S(2)}, u32[]{:S(2)}) collective-permute-start(bf16[256,512]{1,0:T(8,128)(2,1)S(1)} %add_convert_fusion.5), channel_id=1, source_target_pairs={{4,0},{8,4},{12,8},{5,1},{9,5},{13,9},{6,2},{10,6},{14,10},{7,3},{... | collective-permute-start | bytes 786440 | tf_op jit(solution)/shard_map/ppermute | solution.py:16
  143.5 10.6 %collective-permute-start.16 = (bf16[256,512]{1,0:T(8,128)(2,1)}, bf16[256,512]{1,0:T(8,128)(2,1)}, u32[]{:S(2)}, u32[]{:S(2)}) collective-permute-start(bf16[256,512]{1,0:T(8,128)(2,1)} %add_convert_fusion.2), channel_id=1, source_target_pairs={{4,0},{8,4},{12,8},{5,1},{9,5},{13,9},{6,2},{10,6},{14,10},{7,3},{... | collective-permute-start | bytes 786440 | tf_op jit(solution)/shard_map/ppermute | solution.py:16
  145.0 22.0 %copy-start.6 = (bf16[1024,512]{0,1:T(8,128)(2,1)S(1)}, bf16[1024,512]{0,1:T(8,128)(2,1)}, u32[]{:S(2)}) copy-start(bf16[1024,512]{0,1:T(8,128)(2,1)} %copy.30) | copy-start | bytes 3145732
  151.3 10.2 %collective-permute-start.13 = (bf16[256,512]{1,0:T(8,128)(2,1)S(1)}, bf16[256,512]{1,0:T(8,128)(2,1)}, u32[]{:S(2)}, u32[]{:S(2)}) collective-permute-start(bf16[256,512]{1,0:T(8,128)(2,1)S(1)} %add_convert_fusion.4), channel_id=1, source_target_pairs={{4,0},{8,4},{12,8},{5,1},{9,5},{13,9},{6,2},{10,6},{14,10},{7,3},{... | collective-permute-start | bytes 786440 | tf_op jit(solution)/shard_map/ppermute | solution.py:16
  155.9 8.6 %collective-permute-start.17 = (bf16[256,512]{1,0:T(8,128)(2,1)}, bf16[256,512]{1,0:T(8,128)(2,1)}, u32[]{:S(2)}, u32[]{:S(2)}) collective-permute-start(bf16[256,512]{1,0:T(8,128)(2,1)} %add_convert_fusion.1), channel_id=1, source_target_pairs={{4,0},{8,4},{12,8},{5,1},{9,5},{13,9},{6,2},{10,6},{14,10},{7,3},{... | collective-permute-start | bytes 786440 | tf_op jit(solution)/shard_map/ppermute | solution.py:16
  161.3 19.5 %copy-start.1 = (bf16[1,4096,1,512]{3,1,2,0:T(8,128)(2,1)S(1)}, bf16[1,4096,1,512]{3,1,2,0:T(8,128)(2,1)}, u32[]{:S(2)}) copy-start(bf16[1,4096,1,512]{3,1,2,0:T(8,128)(2,1)} %copy-done) | copy-start | bytes 12582916
  162.8 15.2 %collective-permute-start.14 = (bf16[256,512]{1,0:T(8,128)(2,1)S(1)}, bf16[256,512]{1,0:T(8,128)(2,1)S(1)}, u32[]{:S(2)}, u32[]{:S(2)}) collective-permute-start(bf16[256,512]{1,0:T(8,128)(2,1)S(1)} %add_convert_fusion.3), channel_id=1, source_target_pairs={{16,0},{17,1},{18,2},{19,3},{20,4},{21,5},{22,6},{23,7},{24,8},{25... | collective-permute-start | bytes 786440 | tf_op jit(solution)/shard_map/ppermute | solution.py:16
  165.7 15.1 %collective-permute-start.18 = (bf16[256,512]{1,0:T(8,128)(2,1)S(1)}, bf16[256,512]{1,0:T(8,128)(2,1)S(1)}, u32[]{:S(2)}, u32[]{:S(2)}) collective-permute-start(bf16[256,512]{1,0:T(8,128)(2,1)S(1)} %add_convert_fusion), channel_id=1, source_target_pairs={{16,0},{17,1},{18,2},{19,3},{20,4},{21,5},{22,6},{23,7},{24,8},{25... | collective-permute-start | bytes 786440 | tf_op jit(solution)/shard_map/ppermute | solution.py:16
  180.8 0.7 copy-start.10
  180.8 0.8 copy-start.16
  181.6 2.4 %copy-start.2 = (bf16[4096,512]{1,0:T(8,128)(2,1)S(1)}, bf16[4096,512]{1,0:T(8,128)(2,1)}, u32[]{:S(2)}) copy-start(bf16[4096,512]{1,0:T(8,128)(2,1)} %get-tuple-element.53) | copy-start | bytes 12582916 | tf_op jit(solution)/shard_map/cond
  181.6 2.5 %copy-start.17 = (bf16[256,512]{1,0:T(8,128)(2,1)S(1)}, bf16[256,512]{1,0:T(8,128)(2,1)}, u32[]{:S(2)}) copy-start(bf16[256,512]{1,0:T(8,128)(2,1)} %copy-done.16) | copy-start | bytes 786436 | tf_op jit(solution)/shard_map/cond
Sparse Core Ops, SparseCore 0:
  37.8 24.3 all-gather.1
  104.3 37.6 reduce-scatter.2
  187.1 32.3 reduce-scatter.4
where the time goes:
time: 237 us; the launch traced here: 236 us
  local copies, waits for them, and re-layouts  54 us (23%)
  starting transfers between devices  46.5 us (20%)
  waiting for transfers between devices  44.9 us (19%)
  matrix products  42.4 us (18%)
  other arithmetic  28 us (12%)
  between operations  14.2 us (6%)
  blocking collectives  5.76 us (2%)
    ppermute x19, starting transfers between devices, from_behind(): return lax.ppermute(x, axis, pairs)  46.3 us
    reduce_scatter x1, waiting for transfers between devices, per_device(): lax.psum_scatter(partial_grad.astype(jnp.bfloat16), 'mp', scatter_dimensi...  28 us
    slice x1, local copies, waits for them, and re-layouts, per_device(): w_primary = projections[0, :, 0, :]  17.6 us
    ppermute x19, waiting for transfers between devices, from_behind(): return lax.ppermute(x, axis, pairs)  16.8 us
    unnamed x38, local copies, waits for them, and re-layouts  14.4 us
    sub x1, matrix products, per_device(): expo = jnp.exp(scores - row_max)  7.37 us
    psum x1, blocking collectives, per_device(): lax.psum(jnp.sum(summed * own_gain * own_states, axis=-1, keepdims=True),...  5.76 us
    dot_general x1, matrix products, per_device(): jnp.einsum('hqk,khd->qhd', weights_low, all_values, preferred_element_typ...  5.55 us
  transfers between devices with their start and end apart: 22, of which 10 were waited for; matrix products, arithmetic and copies ran while one was open for 36% of the time, Pallas kernels for 0%

commit v1 on v0

--- a/solution.py
+++ b/solution.py
@@ -142,7 +142,10 @@
     ).astype(jnp.float32)
     own_states = lax.dynamic_slice_in_dim(widened, model_index * feature_width, feature_width, 1)
     own_gain = lax.dynamic_slice_in_dim(gain_row, model_index * feature_width, feature_width, 0)
-    row_term = lax.psum(jnp.sum(summed * own_gain * own_states, axis=-1, keepdims=True), "mp")
+    row_term = jnp.sum(
+        lax.all_gather(jnp.sum(summed * own_gain * own_states, axis=-1, keepdims=True), "mp"),
+        axis=0,
+    )
     input_grad = (
         own_gain * summed / spread - own_states * row_term / (full_width * spread**3)
     ).astype(jnp.bfloat16)

time: 237 us -> 237 us (level)
    psum x1 -> x0, blocking collectives: 5.76 us -> none  [per_device(): lax.psum(jnp.sum(summed * own_gain * own_states, axis=-1, keepdims=True),...]
    all_gather x0 -> x1, blocking collectives: none -> 5.07 us  [per_device(): lax.all_gather(jnp.sum(summed * own_gain * own_states, axis=-1, keepdims=...]
where the time goes in v1:
time: 237 us; the launch traced here: 235 us
  local copies, waits for them, and re-layouts  54 us (23%)
  starting transfers between devices  46.5 us (20%)
  waiting for transfers between devices  44.9 us (19%)
  matrix products  42.4 us (18%)
  other arithmetic  28.1 us (12%)
  between operations  14.2 us (6%)
  blocking collectives  5.07 us (2%)
    ppermute x19, starting transfers between devices, from_behind(): return lax.ppermute(x, axis, pairs)  46.3 us
    reduce_scatter x1, waiting for transfers between devices, per_device(): lax.psum_scatter(partial_grad.astype(jnp.bfloat16), 'mp', scatter_dimensi...  28 us
    slice x1, local copies, waits for them, and re-layouts, per_device(): w_primary = projections[0, :, 0, :]  17.6 us
    ppermute x19, waiting for transfers between devices, from_behind(): return lax.ppermute(x, axis, pairs)  16.8 us
    unnamed x38, local copies, waits for them, and re-layouts  14.4 us
    sub x1, matrix products, per_device(): expo = jnp.exp(scores - row_max)  7.37 us
    dot_general x1, matrix products, per_device(): jnp.einsum('hqk,khd->qhd', weights_low, all_values, preferred_element_typ...  5.55 us
    squeeze x3, local copies, waits for them, and re-layouts, per_device(): value_total = arrived[1] + value_parts[offset]  5.32 us
  transfers between devices with their start and end apart: 22, of which 10 were waited for; matrix products, arithmetic and copies ran while one was open for 36% of the time, Pallas kernels for 0%

profile of v1, /device:TPU:0, one launch (start us, length us, event | category | flops | bytes accessed | tf_op | source)
XLA Modules:
  0.0 235.1 jit_solution(8730586750725739785)
XLA Ops:
  7.2 2.1 fusion.2
  9.3 17.6 %fusion.40 = (bf16[1,4096,1,512]{3,2,1,0:T(2,128)(2,1)}, bf16[1,4096,1,512]{3,2,1,0:T(2,128)(2,1)S(1)}) fusion(bf16[1,4096,2,512]{3,2,1,0:T(2,128)(2,1)} %param.13), kind=kLoop, calls=%fused_computation.70 | loop fusion | bytes 16777216 | tf_op jit(solution)/shard_map/slice | solution.py:38
  27.0 3.3 %copy.59 = bf16[1,4096,1,512]{3,1,2,0:T(8,128)(2,1)} copy(bf16[1,4096,1,512]{3,2,1,0:T(2,128)(2,1)S(1)} %get-tuple-element.63) | data formatting | bytes 8388608
  30.2 2.0 fusion.4
  32.3 4.1 %conditional.3 = (bf16[256,512]{1,0:T(8,128)(2,1)S(1)}) conditional(s32[]{:T(128)} %convert_element_type.110, () %tuple.27, (bf16[256,4096]{1,0:T(8,128)(2,1)}, bf16[4096,512]{1,0:T(8,128)(2,1)}) %tuple.58), branch_computations={%region_1.0_spmd, %region_2.0_spmd} | conditional | flops 1073872896 | bytes 6553608 | solution.py:44
  32.3 4.1 %convolution_convert_fusion = bf16[256,512]{1,0:T(8,128)(2,1)S(1)} fusion(bf16[256,4096]{1,0:T(8,128)(2,1)} %get-tuple-element.42, bf16[4096,512]{1,0:T(8,128)(2,1)} %get-tuple-element.43), kind=kOutput, calls=%fused_computation | convolution fusion | flops 1073872896 | bytes 6553600 | tf_op jit(solution)/shard_map/cond/branch_1_fun/dot_general | solution.py:46
  37.7 4.6 %copy.58 = bf16[1,4096,1,512]{3,1,2,0:T(8,128)(2,1)S(1)} copy(bf16[1,4096,1,512]{3,2,1,0:T(2,128)(2,1)} %get-tuple-element.62) | data formatting | bytes 8388608
  45.6 5.0 %collective-permute-start.1 = (bf16[256,512]{1,0:T(8,128)(2,1)S(1)}, bf16[256,512]{1,0:T(8,128)(2,1)S(1)}, u32[]{:S(2)}, u32[]{:S(2)}) collective-permute-start(bf16[256,512]{1,0:T(8,128)(2,1)S(1)} %collective-permute-done), channel_id=1, source_target_pairs={{0,4},{4,8},{8,12},{1,5},{5,9},{9,13},{2,6},{6,10},{10,14},{3,7},{... | collective-permute-start | bytes 786440 | tf_op jit(solution)/shard_map/ppermute | solution.py:16
  50.6 1.5 collective-permute-done.7
  52.0 4.3 %collective-permute-start.8 = (bf16[256,512]{1,0:T(8,128)(2,1)S(1)}, bf16[256,512]{1,0:T(8,128)(2,1)S(1)}, u32[]{:S(2)}, u32[]{:S(2)}) collective-permute-start(bf16[256,512]{1,0:T(8,128)(2,1)S(1)} %collective-permute-done.7), channel_id=1, source_target_pairs={{0,4},{4,8},{8,12},{1,5},{5,9},{9,13},{2,6},{6,10},{10,14},{3,7},{... | collective-permute-start | bytes 786440 | tf_op jit(solution)/shard_map/ppermute | solution.py:16
  57.0 4.0 %collective-permute-start.4 = (s32[1]{0:T(128)}, s32[1]{0:T(128)}, u32[]{:S(2)}, u32[]{:S(2)}) collective-permute-start(s32[1]{0:T(128)} %bitcast.8), channel_id=1, source_target_pairs={{0,4},{4,8},{8,12},{1,5},{5,9},{9,13},{2,6},{6,10},{10,14},{3,7},{... | collective-permute-start | bytes 20 | tf_op jit(solution)/shard_map/ppermute | solution.py:16
  61.0 3.7 %collective-permute-start.2 = (bf16[256,512]{1,0:T(8,128)(2,1)S(1)}, bf16[256,512]{1,0:T(8,128)(2,1)}, u32[]{:S(2)}, u32[]{:S(2)}) collective-permute-start(bf16[256,512]{1,0:T(8,128)(2,1)S(1)} %collective-permute-done.1), channel_id=1, source_target_pairs={{0,4},{4,8},{8,12},{1,5},{5,9},{9,13},{2,6},{6,10},{10,14},{3,7},{... | collective-permute-start | bytes 786440 | tf_op jit(solution)/shard_map/ppermute | solution.py:16
  65.4 2.0 collective-permute-start.9
  68.1 3.2 %collective-permute-start.5 = (s32[1]{0:T(128)}, s32[1]{0:T(128)}, u32[]{:S(2)}, u32[]{:S(2)}) collective-permute-start(s32[1]{0:T(128)} %collective-permute-done.4), channel_id=1, source_target_pairs={{0,4},{4,8},{8,12},{1,5},{5,9},{9,13},{2,6},{6,10},{10,14},{3,7},{... | collective-permute-start | bytes 20 | tf_op jit(solution)/shard_map/ppermute | solution.py:16
  71.9 3.8 %collective-permute-start.3 = (bf16[256,512]{1,0:T(8,128)(2,1)}, bf16[256,512]{1,0:T(8,128)(2,1)S(1)}, u32[]{:S(2)}, u32[]{:S(2)}) collective-permute-start(bf16[256,512]{1,0:T(8,128)(2,1)} %collective-permute-done.2), channel_id=1, source_target_pairs={{0,4},{4,8},{8,12},{1,5},{5,9},{9,13},{2,6},{6,10},{10,14},{3,7},{... | collective-permute-start | bytes 786440 | tf_op jit(solution)/shard_map/ppermute | solution.py:16
  76.5 4.2 %collective-permute-start.6 = (s32[1]{0:T(128)}, s32[1]{0:T(128)}, u32[]{:S(2)}, u32[]{:S(2)}) collective-permute-start(s32[1]{0:T(128)} %collective-permute-done.5), channel_id=1, source_target_pairs={{0,4},{4,8},{8,12},{1,5},{5,9},{9,13},{2,6},{6,10},{10,14},{3,7},{... | collective-permute-start | bytes 20 | tf_op jit(solution)/shard_map/ppermute | solution.py:16
  80.7 2.9 %collective-permute-start.10 = (bf16[256,512]{1,0:T(8,128)(2,1)}, bf16[256,512]{1,0:T(8,128)(2,1)}, u32[]{:S(2)}, u32[]{:S(2)}) collective-permute-start(bf16[256,512]{1,0:T(8,128)(2,1)} %collective-permute-done.9), channel_id=1, source_target_pairs={{0,4},{4,8},{8,12},{1,5},{5,9},{9,13},{2,6},{6,10},{10,14},{3,7},{... | collective-permute-start | bytes 786440 | tf_op jit(solution)/shard_map/ppermute | solution.py:16
  89.7 7.4 %fusion.44 = (f32[8,256]{1,0:T(8,128)S(1)}, f32[8,256,1024]{2,1,0:T(8,128)}) fusion(pred[1024]{0:T(1024)(128)(4,1)S(1)} %pad_add_fusion, bf16[256,8,64]{0,2,1:T(8,128)(2,1)S(1)} %bitcast.111, bf16[1024,8,64]{0,2,1:T(8,128)(2,1)} %bitcast.102), kind=kOutput, calls=%fused_computation.74 | convolution fusion | flops 276825088 | bytes 9708544 | tf_op jit(solution)/shard_map/sub | solution.py:74
  97.0 5.6 %fusion.25 = bf16[256,8,64]{0,2,1:T(8,128)(2,1)} fusion(bf16[1024,8,64]{0,2,1:T(8,128)(2,1)S(1)} %bitcast.113, f32[8,256,1024]{2,1,0:T(8,128)} %get-tuple-element.75, f32[8,256]{1,0:T(8,128)S(1)} %get-tuple-element.74), kind=kOutput, calls=%fused_computation.35 | convolution fusion | flops 272760832 | bytes 9707520 | tf_op jit(solution)/shard_map/hqk,khd->qhd/dot_general | solution.py:78
  102.6 1.6 conditional.4
  102.6 1.6 broadcast.54
  104.3 4.8 %fusion.29 = bf16[256,512]{1,0:T(8,128)(2,1)} fusion(bf16[256,4096]{1,0:T(8,128)(2,1)} %all-gather.4.cloned.1.call-done, bf16[4096,512]{1,0:T(8,128)(2,1)} %bitcast.98, pred[256]{0:T(512)(128)(4,1)S(1)} %iota_compare_fusion), kind=kOutput, calls=%fused_computation.37 | convolution fusion | flops 1074003968 | bytes 6553856 | tf_op jit(solution)/shard_map/dot_general | solution.py:94
  109.1 1.8 copy.45
  110.9 5.1 %multiply_reduce_fusion = (f32[8,256]{1,0:T(8,128)S(1)}, f32[8,256,1024]{2,1,0:T(8,128)S(1)}) fusion(f32[8,256,1024]{2,1,0:T(8,128)} %get-tuple-element.75, f32[8,256]{1,0:T(8,128)S(1)} %get-tuple-element.74, bf16[256,8,64]{0,2,1:T(8,128)(2,1)} %bitcast.118, bf16[1024,8,64]{0,2,1:T(8,128)(2,1)S(1)} %bitcast.114), kind=kOutput, calls=%fused_computation.6 | convolution fusion | flops 274724864 | bytes 18104320 | tf_op jit(solution)/shard_map/qhd,khd->hqk/dot_general | solution.py:102
  118.5 2.0 copy-done.3
  124.3 4.5 %fusion.15 = f32[1024,8,64]{0,2,1:T(8,128)S(1)} fusion(bf16[256,8,64]{0,2,1:T(8,128)(2,1)S(1)} %bitcast.119, f32[8,256,1024]{2,1,0:T(8,128)} %get-tuple-element.75, f32[8,256]{1,0:T(8,128)S(1)} %get-tuple-element.74), kind=kOutput, calls=%fused_computation.29 | convolution fusion | flops 272629760 | bytes 10756096 | tf_op jit(solution)/shard_map/hqk,qhd->khd/dot_general | solution.py:119
  132.5 2.5 %fusion.42 = (f32[256,8,64]{0,2,1:T(8,128)S(1)}, f32[256,8,64]{0,2,1:T(8,128)}, f32[256,8,64]{0,2,1:T(8,128)}) fusion(f32[1024,8,64]{0,2,1:T(8,128)} %copy-done.5), kind=kLoop, calls=%fused_computation.72 | loop fusion | bytes 3145728 | tf_op jit(solution)/shard_map/slice | solution.py:129
  139.9 1.8 collective-permute-done.15
  141.8 1.7 add_convert_fusion.2
  143.5 1.5 collective-permute-start.16
  145.0 2.2 copy.48
  147.2 2.0 copy.52
  152.6 1.5 collective-permute-done.16
  154.1 1.9 add_convert_fusion.1
  157.2 2.0 copy.49
  159.3 2.0 copy.53
  167.0 3.6 %fusion.28 = bf16[256,8,64]{0,2,1:T(8,128)(2,1)S(1)} fusion(bf16[1024,8,64]{0,2,1:T(8,128)(2,1)S(1)} %bitcast.103, bf16[8,256,1024]{2,1,0:T(8,128)(2,1)} %copy-done.3), kind=kOutput, calls=%fused_computation.36 | convolution fusion | flops 268697600 | bytes 5505024 | tf_op jit(solution)/shard_map/hqk,khd->qhd/dot_general | solution.py:110
  170.6 7.4 %collective-permute-done.14 = bf16[256,512]{1,0:T(8,128)(2,1)S(1)} collective-permute-done((bf16[256,512]{1,0:T(8,128)(2,1)S(1)}, bf16[256,512]{1,0:T(8,128)(2,1)S(1)}, u32[]{:S(2)}, u32[]{:S(2)}) %collective-permute-start.14) | collective-permute-done | bytes 262176 | tf_op jit(solution)/shard_map/ppermute | solution.py:16
  178.0 2.8 %collective-permute-done.18 = bf16[256,512]{1,0:T(8,128)(2,1)S(1)} collective-permute-done((bf16[256,512]{1,0:T(8,128)(2,1)S(1)}, bf16[256,512]{1,0:T(8,128)(2,1)S(1)}, u32[]{:S(2)}, u32[]{:S(2)}) %collective-permute-start.18) | collective-permute-done | bytes 262176 | tf_op jit(solution)/shard_map/ppermute | solution.py:16
  180.8 6.1 %conditional.5 = (bf16[256,4096]{1,0:T(8,128)(2,1)}) conditional(s32[]{:T(128)} %convert_element_type.110, (bf16[256,8,64]{0,2,1:T(8,128)(2,1)S(1)}, bf16[4096,512]{1,0:T(8,128)(2,1)S(1)}) %tuple.56, (bf16[256,512]{1,0:T(8,128)(2,1)S(1)}, bf16[4096,512]{1,0:T(8,128)(2,1)S(1)}, bf16[256,512]{1,0:T(8,128)(2,1)S(1)}, ...), branch_computations={%region_9.10_spmd, %region_10.11_spmd} | conditional | flops 2149580800 | bytes 39321720 | solution.py:134
  181.6 2.4 %fusion.46 = f32[256,4096]{1,0:T(8,128)S(1)} fusion(bf16[256,512]{1,0:T(8,128)(2,1)} %copy-done.10, bf16[4096,512]{1,0:T(8,128)(2,1)S(1)} %get-tuple-element.51), kind=kOutput, calls=%fused_computation.76 | convolution fusion | flops 1073741824 | bytes 8650752 | tf_op jit(solution)/shard_map/cond/branch_1_fun/dot_general | solution.py:26
  184.1 2.8 %convolution_add_fusion = bf16[256,4096]{1,0:T(8,128)(2,1)} fusion(f32[256,4096]{1,0:T(8,128)S(1)} %fusion.46, bf16[256,512]{1,0:T(8,128)(2,1)S(1)} %copy-done.17, bf16[4096,512]{1,0:T(8,128)(2,1)S(1)} %copy-done.2), kind=kOutput, calls=%fused_computation.1 | convolution fusion | flops 1075838976 | bytes 10747904 | tf_op jit(solution)/shard_map/cond/branch_1_fun/dot_general | solution.py:26
  186.9 2.5 %convert_element_type.106 = f32[1,256,4096]{2,1,0:T(8,128)} convert(bf16[1,256,4096]{2,1,0:T(8,128)(2,1)S(1)} %copy-done.4) | non-fusion elementwise | flops 1048576 | bytes 6291456 | tf_op jit(solution)/shard_map/convert_element_type | solution.py:20
  189.4 2.0 select_bitcast_fusion
  191.5 28.0 %reduce-scatter.5.cloned.1.call-done = bf16[256,1024]{1,0:T(8,128)(2,1)} async-done(((bf16[256,4096]{1,0:T(8,128)(2,1)}), bf16[256,1024]{1,0:T(8,128)(2,1)}) %reduce-scatter.5.cloned.1.call-update) | async-done | bytes 524304 | tf_op jit(solution)/shard_map/reduce_scatter | solution.py:140
  219.5 1.6 fusion.30
  221.1 5.1 %all-gather.1 = f32[4,1,256]{2,1,0:T(1,128)S(1)} all-gather(f32[1,1,256]{2,1,0:T(1,128)S(1)} %bitcast.124), channel_id=2, replica_groups=mesh['segment'=2,'blk'=4,'mp'=4] {'mp'}, dimensions={0}, use_global_device_ids=true | all-gather | bytes 5120 | tf_op jit(solution)/shard_map/all_gather | solution.py:146
  226.2 2.4 %fusion.36 = bf16[1,256,1024]{2,1,0:T(8,128)(2,1)} fusion(f32[256]{0:T(256)S(1)} %get-tuple-element.70, f32[256]{0:T(256)S(1)} %reduce.1, f32[1,256,4096]{2,1,0:T(8,128)} %convert_element_type.106, s32[]{:T(128)S(6)} %select_n.27, f32[256]{0:T(256)S(1)} %get-tuple-element.71, bf16[256,1024]{1,0:T(8,128)(2,1)} %reduce-scatter.5.cloned.1.call-done, ...), kind=kLoop, calls=%fused_computation.57 | loop fusion | flops 1835008 | bytes 2104324 | tf_op jit(solution)/shard_map/broadcast_in_dim | solution.py:152
  (105 shorter events, 40.1 us)
Async XLA Ops:
  7.2 97.1 %all-gather.4.cloned.1.call-start = ((), (), s32[]{:S(2)}) async-start(), calls=%async_computation.3 | async-start | bytes 2621440 | tf_op jit(solution)/shard_map/all_gather | solution.py:95
  26.9 3.3 %copy-start.4 = (bf16[1,256,4096]{2,1,0:T(8,128)(2,1)S(1)}, bf16[1,256,4096]{2,1,0:T(8,128)(2,1)}, u32[]{:S(2)}) copy-start(bf16[1,256,4096]{2,1,0:T(8,128)(2,1)} %param.11) | copy-start | bytes 6291460
  26.9 3.3 %copy-start.18 = (f32[1,4096]{1,0:T(1,128)S(1)}, f32[1,4096]{1,0:T(1,128)}, u32[]{:S(2)}) copy-start(f32[1,4096]{1,0:T(1,128)} %param.12) | copy-start | bytes 49156
  36.3 9.2 %collective-permute-start = (bf16[256,512]{1,0:T(8,128)(2,1)S(1)}, bf16[256,512]{1,0:T(8,128)(2,1)S(1)}, u32[]{:S(2)}, u32[]{:S(2)}) collective-permute-start(bf16[256,512]{1,0:T(8,128)(2,1)S(1)} %get-tuple-element.78), channel_id=1, source_target_pairs={{0,16},{1,17},{2,18},{3,19},{4,20},{5,21},{6,22},{7,23},{8,24},{9,... | collective-permute-start | bytes 786440 | tf_op jit(solution)/shard_map/ppermute | solution.py:16
  37.7 151.8 %reduce-scatter.3.cloned.1.call-start = ((), (), s32[]{:S(2)}) async-start(), calls=%async_computation.2 | async-start | bytes 2621440 | tf_op jit(solution)/shard_map/reduce_scatter | solution.py:89
  42.3 1.9 copy-start
  42.4 14.0 %copy-start.19 = (s32[2,1]{0,1:T(1,128)S(1)}, s32[2,1]{0,1:T(1,128)}, u32[]{:S(2)}) copy-start(s32[2,1]{0,1:T(1,128)} %param.14) | copy-start | bytes 28
  44.3 7.8 %collective-permute-start.7 = (bf16[256,512]{1,0:T(8,128)(2,1)S(1)}, bf16[256,512]{1,0:T(8,128)(2,1)S(1)}, u32[]{:S(2)}, u32[]{:S(2)}) collective-permute-start(bf16[256,512]{1,0:T(8,128)(2,1)S(1)} %fusion.22), channel_id=1, source_target_pairs={{0,16},{1,17},{2,18},{3,19},{4,20},{5,21},{6,22},{7,23},{8,24},{9,... | collective-permute-start | bytes 786440 | tf_op jit(solution)/shard_map/ppermute | solution.py:16
  45.6 38.7 %copy-start.12 = (bf16[256,512]{1,0:T(8,128)(2,1)}, bf16[256,512]{1,0:T(8,128)(2,1)S(1)}, u32[]{:S(2)}) copy-start(bf16[256,512]{1,0:T(8,128)(2,1)S(1)} %collective-permute-done) | copy-start | bytes 786436
  45.6 15.4 %collective-permute-start.1 = (bf16[256,512]{1,0:T(8,128)(2,1)S(1)}, bf16[256,512]{1,0:T(8,128)(2,1)S(1)}, u32[]{:S(2)}, u32[]{:S(2)}) collective-permute-start(bf16[256,512]{1,0:T(8,128)(2,1)S(1)} %collective-permute-done), channel_id=1, source_target_pairs={{0,4},{4,8},{8,12},{1,5},{5,9},{9,13},{2,6},{6,10},{10,14},{3,7},{... | collective-permute-start | bytes 786440 | tf_op jit(solution)/shard_map/ppermute | solution.py:16
  52.0 15.9 %copy-start.13 = (bf16[256,512]{1,0:T(8,128)(2,1)}, bf16[256,512]{1,0:T(8,128)(2,1)S(1)}, u32[]{:S(2)}) copy-start(bf16[256,512]{1,0:T(8,128)(2,1)S(1)} %collective-permute-done.7) | copy-start | bytes 786436
  52.0 13.3 %collective-permute-start.8 = (bf16[256,512]{1,0:T(8,128)(2,1)S(1)}, bf16[256,512]{1,0:T(8,128)(2,1)S(1)}, u32[]{:S(2)}, u32[]{:S(2)}) collective-permute-start(bf16[256,512]{1,0:T(8,128)(2,1)S(1)} %collective-permute-done.7), channel_id=1, source_target_pairs={{0,4},{4,8},{8,12},{1,5},{5,9},{9,13},{2,6},{6,10},{10,14},{3,7},{... | collective-permute-start | bytes 786440 | tf_op jit(solution)/shard_map/ppermute | solution.py:16
  57.0 11.1 %collective-permute-start.4 = (s32[1]{0:T(128)}, s32[1]{0:T(128)}, u32[]{:S(2)}, u32[]{:S(2)}) collective-permute-start(s32[1]{0:T(128)} %bitcast.8), channel_id=1, source_target_pairs={{0,4},{4,8},{8,12},{1,5},{5,9},{9,13},{2,6},{6,10},{10,14},{3,7},{... | collective-permute-start | bytes 20 | tf_op jit(solution)/shard_map/ppermute | solution.py:16
  61.0 23.3 %copy-start.15 = (bf16[256,512]{1,0:T(8,128)(2,1)}, bf16[256,512]{1,0:T(8,128)(2,1)S(1)}, u32[]{:S(2)}) copy-start(bf16[256,512]{1,0:T(8,128)(2,1)S(1)} %collective-permute-done.1) | copy-start | bytes 786436
  61.0 10.9 %collective-permute-start.2 = (bf16[256,512]{1,0:T(8,128)(2,1)S(1)}, bf16[256,512]{1,0:T(8,128)(2,1)}, u32[]{:S(2)}, u32[]{:S(2)}) collective-permute-start(bf16[256,512]{1,0:T(8,128)(2,1)S(1)} %collective-permute-done.1), channel_id=1, source_target_pairs={{0,4},{4,8},{8,12},{1,5},{5,9},{9,13},{2,6},{6,10},{10,14},{3,7},{... | collective-permute-start | bytes 786440 | tf_op jit(solution)/shard_map/ppermute | solution.py:16
  65.4 18.9 %copy-start.14 = (bf16[256,512]{1,0:T(8,128)(2,1)}, bf16[256,512]{1,0:T(8,128)(2,1)S(1)}, u32[]{:S(2)}) copy-start(bf16[256,512]{1,0:T(8,128)(2,1)S(1)} %collective-permute-done.8) | copy-start | bytes 786436
  65.4 15.3 %collective-permute-start.9 = (bf16[256,512]{1,0:T(8,128)(2,1)S(1)}, bf16[256,512]{1,0:T(8,128)(2,1)}, u32[]{:S(2)}, u32[]{:S(2)}) collective-permute-start(bf16[256,512]{1,0:T(8,128)(2,1)S(1)} %collective-permute-done.8), channel_id=1, source_target_pairs={{0,4},{4,8},{8,12},{1,5},{5,9},{9,13},{2,6},{6,10},{10,14},{3,7},{... | collective-permute-start | bytes 786440 | tf_op jit(solution)/shard_map/ppermute | solution.py:16
  68.1 7.7 %collective-permute-start.5 = (s32[1]{0:T(128)}, s32[1]{0:T(128)}, u32[]{:S(2)}, u32[]{:S(2)}) collective-permute-start(s32[1]{0:T(128)} %collective-permute-done.4), channel_id=1, source_target_pairs={{0,4},{4,8},{8,12},{1,5},{5,9},{9,13},{2,6},{6,10},{10,14},{3,7},{... | collective-permute-start | bytes 20 | tf_op jit(solution)/shard_map/ppermute | solution.py:16
  71.9 12.4 %collective-permute-start.3 = (bf16[256,512]{1,0:T(8,128)(2,1)}, bf16[256,512]{1,0:T(8,128)(2,1)S(1)}, u32[]{:S(2)}, u32[]{:S(2)}) collective-permute-start(bf16[256,512]{1,0:T(8,128)(2,1)} %collective-permute-done.2), channel_id=1, source_target_pairs={{0,4},{4,8},{8,12},{1,5},{5,9},{9,13},{2,6},{6,10},{10,14},{3,7},{... | collective-permute-start | bytes 786440 | tf_op jit(solution)/shard_map/ppermute | solution.py:16
  76.5 7.1 %collective-permute-start.6 = (s32[1]{0:T(128)}, s32[1]{0:T(128)}, u32[]{:S(2)}, u32[]{:S(2)}) collective-permute-start(s32[1]{0:T(128)} %collective-permute-done.5), channel_id=1, source_target_pairs={{0,4},{4,8},{8,12},{1,5},{5,9},{9,13},{2,6},{6,10},{10,14},{3,7},{... | collective-permute-start | bytes 20 | tf_op jit(solution)/shard_map/ppermute | solution.py:16
  80.7 6.4 %collective-permute-start.10 = (bf16[256,512]{1,0:T(8,128)(2,1)}, bf16[256,512]{1,0:T(8,128)(2,1)}, u32[]{:S(2)}, u32[]{:S(2)}) collective-permute-start(bf16[256,512]{1,0:T(8,128)(2,1)} %collective-permute-done.9), channel_id=1, source_target_pairs={{0,4},{4,8},{8,12},{1,5},{5,9},{9,13},{2,6},{6,10},{10,14},{3,7},{... | collective-permute-start | bytes 786440 | tf_op jit(solution)/shard_map/ppermute | solution.py:16
  89.7 7.4 %copy-start.9 = (bf16[1024,512]{0,1:T(8,128)(2,1)S(1)}, bf16[1024,512]{0,1:T(8,128)(2,1)}, u32[]{:S(2)}) copy-start(bf16[1024,512]{0,1:T(8,128)(2,1)} %copy.41) | copy-start | bytes 3145732
  104.2 115.3 %reduce-scatter.5.cloned.1.call-start = ((), (), s32[]{:S(2)}) async-start(), calls=%async_computation.4 | async-start | bytes 2621440 | tf_op jit(solution)/shard_map/reduce_scatter | solution.py:140
  110.9 5.1 %slice-start = ((s8[8388608]{0:T(1024)(128)(4,1)}), s8[4194304]{0:T(1024)(128)(4,1)S(1)}, s32[]{:S(2)}) async-start(s8[8388608]{0:T(1024)(128)(4,1)} %bitcast.100), calls=%async_computation.5 | async-start | bytes 8388608
  110.9 6.3 %slice-start.1 = ((s8[8388608]{0:T(1024)(128)(4,1)}), s8[4194304]{0:T(1024)(128)(4,1)S(1)}, s32[]{:S(2)}) async-start(s8[8388608]{0:T(1024)(128)(4,1)} %bitcast.100), calls=%async_computation.6 | async-start | bytes 8388608
  118.5 2.0 copy-start.3
  120.5 3.8 %copy-start.11 = (bf16[256,512]{0,1:T(8,128)(2,1)S(1)}, bf16[256,512]{0,1:T(8,128)(2,1)}, u32[]{:S(2)}) copy-start(bf16[256,512]{0,1:T(8,128)(2,1)} %copy.45) | copy-start | bytes 786436
  121.3 1.4 copy-start.5
  122.9 14.7 %collective-permute-start.11 = (bf16[256,512]{1,0:T(8,128)(2,1)S(1)}, bf16[256,512]{1,0:T(8,128)(2,1)}, u32[]{:S(2)}, u32[]{:S(2)}) collective-permute-start(bf16[256,512]{1,0:T(8,128)(2,1)S(1)} %copy.46), channel_id=1, source_target_pairs={{4,0},{8,4},{12,8},{5,1},{9,5},{13,9},{6,2},{10,6},{14,10},{7,3},{... | collective-permute-start | bytes 786440 | tf_op jit(solution)/shard_map/ppermute | solution.py:16
  128.8 1.4 copy-start.7
  131.0 3.9 %copy-start.8 = (f32[1024,8,64]{0,2,1:T(8,128)S(1)}, f32[1024,8,64]{0,2,1:T(8,128)}, u32[]{:S(2)}) copy-start(f32[1024,8,64]{0,2,1:T(8,128)} %copy-done.7) | copy-start | bytes 6291460
  131.0 10.7 %collective-permute-start.15 = (bf16[256,512]{1,0:T(8,128)(2,1)}, bf16[256,512]{1,0:T(8,128)(2,1)}, u32[]{:S(2)}, u32[]{:S(2)}) collective-permute-start(bf16[256,512]{1,0:T(8,128)(2,1)} %copy.50), channel_id=1, source_target_pairs={{4,0},{8,4},{12,8},{5,1},{9,5},{13,9},{6,2},{10,6},{14,10},{7,3},{... | collective-permute-start | bytes 786440 | tf_op jit(solution)/shard_map/ppermute | solution.py:16
  138.6 11.5 %collective-permute-start.12 = (bf16[256,512]{1,0:T(8,128)(2,1)S(1)}, bf16[256,512]{1,0:T(8,128)(2,1)}, u32[]{:S(2)}, u32[]{:S(2)}) collective-permute-start(bf16[256,512]{1,0:T(8,128)(2,1)S(1)} %add_convert_fusion.5), channel_id=1, source_target_pairs={{4,0},{8,4},{12,8},{5,1},{9,5},{13,9},{6,2},{10,6},{14,10},{7,3},{... | collective-permute-start | bytes 786440 | tf_op jit(solution)/shard_map/ppermute | solution.py:16
  143.5 10.6 %collective-permute-start.16 = (bf16[256,512]{1,0:T(8,128)(2,1)}, bf16[256,512]{1,0:T(8,128)(2,1)}, u32[]{:S(2)}, u32[]{:S(2)}) collective-permute-start(bf16[256,512]{1,0:T(8,128)(2,1)} %add_convert_fusion.2), channel_id=1, source_target_pairs={{4,0},{8,4},{12,8},{5,1},{9,5},{13,9},{6,2},{10,6},{14,10},{7,3},{... | collective-permute-start | bytes 786440 | tf_op jit(solution)/shard_map/ppermute | solution.py:16
  145.0 22.0 %copy-start.6 = (bf16[1024,512]{0,1:T(8,128)(2,1)S(1)}, bf16[1024,512]{0,1:T(8,128)(2,1)}, u32[]{:S(2)}) copy-start(bf16[1024,512]{0,1:T(8,128)(2,1)} %copy.44) | copy-start | bytes 3145732
  151.3 10.2 %collective-permute-start.13 = (bf16[256,512]{1,0:T(8,128)(2,1)S(1)}, bf16[256,512]{1,0:T(8,128)(2,1)}, u32[]{:S(2)}, u32[]{:S(2)}) collective-permute-start(bf16[256,512]{1,0:T(8,128)(2,1)S(1)} %add_convert_fusion.4), channel_id=1, source_target_pairs={{4,0},{8,4},{12,8},{5,1},{9,5},{13,9},{6,2},{10,6},{14,10},{7,3},{... | collective-permute-start | bytes 786440 | tf_op jit(solution)/shard_map/ppermute | solution.py:16
  155.9 8.6 %collective-permute-start.17 = (bf16[256,512]{1,0:T(8,128)(2,1)}, bf16[256,512]{1,0:T(8,128)(2,1)}, u32[]{:S(2)}, u32[]{:S(2)}) collective-permute-start(bf16[256,512]{1,0:T(8,128)(2,1)} %add_convert_fusion.1), channel_id=1, source_target_pairs={{4,0},{8,4},{12,8},{5,1},{9,5},{13,9},{6,2},{10,6},{14,10},{7,3},{... | collective-permute-start | bytes 786440 | tf_op jit(solution)/shard_map/ppermute | solution.py:16
  161.3 19.5 %copy-start.1 = (bf16[1,4096,1,512]{3,1,2,0:T(8,128)(2,1)S(1)}, bf16[1,4096,1,512]{3,1,2,0:T(8,128)(2,1)}, u32[]{:S(2)}) copy-start(bf16[1,4096,1,512]{3,1,2,0:T(8,128)(2,1)} %copy-done) | copy-start | bytes 12582916
  162.8 15.2 %collective-permute-start.14 = (bf16[256,512]{1,0:T(8,128)(2,1)S(1)}, bf16[256,512]{1,0:T(8,128)(2,1)S(1)}, u32[]{:S(2)}, u32[]{:S(2)}) collective-permute-start(bf16[256,512]{1,0:T(8,128)(2,1)S(1)} %add_convert_fusion.3), channel_id=1, source_target_pairs={{16,0},{17,1},{18,2},{19,3},{20,4},{21,5},{22,6},{23,7},{24,8},{25... | collective-permute-start | bytes 786440 | tf_op jit(solution)/shard_map/ppermute | solution.py:16
  165.7 15.1 %collective-permute-start.18 = (bf16[256,512]{1,0:T(8,128)(2,1)S(1)}, bf16[256,512]{1,0:T(8,128)(2,1)S(1)}, u32[]{:S(2)}, u32[]{:S(2)}) collective-permute-start(bf16[256,512]{1,0:T(8,128)(2,1)S(1)} %add_convert_fusion), channel_id=1, source_target_pairs={{16,0},{17,1},{18,2},{19,3},{20,4},{21,5},{22,6},{23,7},{24,8},{25... | collective-permute-start | bytes 786440 | tf_op jit(solution)/shard_map/ppermute | solution.py:16
  180.8 0.7 copy-start.10
  180.8 0.8 copy-start.16
  181.6 2.4 %copy-start.2 = (bf16[4096,512]{1,0:T(8,128)(2,1)S(1)}, bf16[4096,512]{1,0:T(8,128)(2,1)}, u32[]{:S(2)}) copy-start(bf16[4096,512]{1,0:T(8,128)(2,1)} %get-tuple-element.53) | copy-start | bytes 12582916 | tf_op jit(solution)/shard_map/cond
  181.6 2.5 %copy-start.17 = (bf16[256,512]{1,0:T(8,128)(2,1)S(1)}, bf16[256,512]{1,0:T(8,128)(2,1)}, u32[]{:S(2)}) copy-start(bf16[256,512]{1,0:T(8,128)(2,1)} %copy-done.16) | copy-start | bytes 786436 | tf_op jit(solution)/shard_map/cond
Sparse Core Ops, SparseCore 0:
  37.8 24.3 all-gather.3
  104.3 37.6 reduce-scatter.2
  187.1 32.3 reduce-scatter.4
